TPU v7x, 256 devices: a whole 4x4x8 slice. The times are simulated.
256 devices in a mesh: dom: 64 (over z, x, core), grp: 4 (over y).
Axes of the slice: x: 4, y: 4, z: 8, core: 2. Of those that a mesh axis runs over, the one named last changes fastest.
Arguments:
- blocks: bfloat16 [12288, 6, 128, 128], P(('dom', 'grp')), may hold values from -0.21875 to 0.21875
- local_cols: int32 [12288, 4], P(('dom', 'grp')), may hold values from 0 to 191
- remote_refs: int32 [12288, 2], P(('dom', 'grp')), may hold values from 0 to 191
- send_blocks: int32 [64, 4, 64, 3], P('dom', 'grp'), may hold values from 0 to 47
- send_counts: int32 [64, 4, 64], P('dom', 'grp'), may hold values from 0 to 3
- probes: bfloat16 [64, 1572864], P(None, ('dom', 'grp')), may hold values from -6 to 6
Outputs:
- moments: float32 [3, 1572864], P(None, ('dom', 'grp'))
All inputs are finite; a program needn't handle non-finite values.
Results may differ from a plain program's by a relative error of at most 0.00064.
Values may be sent and summed in bfloat16 or wider, within the bound.
No kernel may reach another device: no remote copies, remote signals or barrier semaphores. Data moves between devices by JAX's collectives and lax.ppermute only.
A program may use at most 64 MiB of HBM per device.

v0:
```python
import math
import jax
import jax.numpy as jnp
from jax import lax
from jax.sharding import PartitionSpec as P

PROBES = 64
LOCAL = 4
KMOM = 256


def jackson(order, total):
    angle = math.pi / (total + 1)
    return (
        (total - order + 1) * math.cos(order * angle) + math.sin(order * angle) / math.tan(angle)
    ) / (total + 1)


def send_boundary(own, send_list, live):
    outgoing = jnp.take(own, send_list, axis=1)
    outgoing = jnp.where(live[None, :, :, None], outgoing, jnp.zeros_like(outgoing))
    received = lax.all_to_all(outgoing, "dom", split_axis=1, concat_axis=1, tiled=True)
    return received.reshape(own.shape[0], -1, own.shape[2])


def on_device(blocks, local_cols, remote_refs, send_blocks, send_counts, probes):
    rows_here = blocks.shape[0]
    size_block = blocks.shape[2]
    probe_count = probes.shape[0]
    local_blocks = blocks[:, :LOCAL]
    remote_blocks = blocks[:, LOCAL:]
    send_list = send_blocks[0, 0]
    slot_index = jnp.arange(send_list.shape[1], dtype=jnp.int32)
    live = slot_index[None, :] < send_counts[0, 0][:, None]

    def local_part(own):
        panel_all = lax.all_gather(own, "grp", axis=1, tiled=True)
        picked = jnp.take(panel_all, local_cols, axis=1)
        return jnp.einsum(
            "rjab,prjb->pra", local_blocks, picked, preferred_element_type=jnp.float32
        )

    def remote_part(received):
        picked = jnp.take(received, remote_refs, axis=1)
        return jnp.einsum(
            "rjab,prjb->pra", remote_blocks, picked, preferred_element_type=jnp.float32
        )

    def apply_op(field):
        own = field.reshape(probe_count, rows_here, size_block)
        local_sum = local_part(own)
        received = send_boundary(own, send_list, live)
        result = local_sum + remote_part(received)
        return result.reshape(probe_count, rows_here * size_block)

    first = apply_op(probes).astype(jnp.bfloat16)
    base = probes.astype(jnp.float32)
    second = 2.0 * apply_op(first) - base
    norm = 1.0 / math.sqrt(PROBES)
    moment_zero = jackson(0, KMOM) * norm * jnp.sum(base * base, axis=0)
    moment_one = 2.0 * jackson(1, KMOM) * norm * jnp.sum(base * first.astype(jnp.float32), axis=0)
    moment_two = 2.0 * jackson(2, KMOM) * norm * jnp.sum(base * second, axis=0)
    return jnp.stack([moment_zero, moment_one, moment_two], axis=0)


def solution(mesh):
    in_specs = (
        P(("dom", "grp"), None, None, None),
        P(("dom", "grp"), None),
        P(("dom", "grp"), None),
        P("dom", "grp", None, None),
        P("dom", "grp", None),
        P(None, ("dom", "grp")),
    )
    out_specs = P(None, ("dom", "grp"))
    return jax.shard_map(
        on_device, mesh=mesh, in_specs=in_specs, out_specs=out_specs, check_vma=False
    )
```

profile of v0, /device:TPU:16, one launch (start us, length us, event | category | flops | bytes accessed | tf_op | source)
XLA Modules:
  0.0 208.0 jit_solution(10266669360849559524)
XLA Ops:
  6.5 0.7 compare_select_fusion
  7.2 0.7 compare_and_fusion.1
  7.9 1.3 copy_bitcast_fusion
  9.4 0.1 reshape.151
  9.5 0.1 copy.51
  9.6 0.7 iota_compare_fusion
  10.4 2.7 %gather_fusion.1 = bf16[192,64,128]{2,1,0:T(8,128)(2,1)} fusion(bf16[64,48,128]{2,0,1:T(8,128)(2,1)S(1)} %copy_bitcast_fusion, s32[1024]{0:T(1024)S(1)} %pad_clamp_fusion.1), kind=kCustom, calls=%fused_computation.1.clone | custom fusion | bytes 6292224 | tf_op jit(solution)/shard_map/jit(_take)/gather | solution.py:20
  13.1 3.3 %bitcast_select_fusion.1 = bf16[64,64,3,128]{3,0,2,1:T(8,128)(2,1)} fusion(bf16[64,3,64,128]{3,2,1,0:T(8,128)(2,1)} %bitcast.78, pred[64,3]{1,0:T(8,128)(4,1)S(1)} %copy.51, pred[64,3]{1,0:T(8,128)(4,1)S(1)} %iota_compare_fusion), kind=kLoop, calls=%fused_computation.12 | loop fusion | flops 3145728 | bytes 6291840 | tf_op jit(solution)/shard_map/jit(_where)/select_n | solution.py:21
  16.5 12.1 %all-to-all-start = ((bf16[64,64,3,128]{3,0,2,1:T(8,128)(2,1)}), bf16[64,64,3,128]{3,0,2,1:T(8,128)(2,1)S(1)}, u32[]{:S(2)}, u32[]{:S(2)}) async-start(bf16[64,64,3,128]{3,0,2,1:T(8,128)(2,1)} %bitcast_select_fusion.1), calls=%async_computation | async-start | bytes 6291456 | tf_op jit(solution)/shard_map/all_to_all | solution.py:22
  28.6 0.7 all-gather.3.cloned.1.call-update
  29.4 0.1 reshape.155
  29.6 0.1 reshape.147
  29.7 0.1 copy.47
  29.9 0.1 copy.50
  30.0 43.3 %all-gather.3.cloned.1.call-done = bf16[64,192,128]{2,0,1:T(8,128)(2,1)} async-done(((bf16[64,48,128]{2,0,1:T(8,128)(2,1)}), bf16[64,192,128]{2,0,1:T(8,128)(2,1)}) %all-gather.3.cloned.1.call-update) | async-done | bytes 3145744 | tf_op jit(solution)/shard_map/all_gather | solution.py:37
  73.3 4.7 %gather_fusion = bf16[192,64,128]{2,1,0:T(8,128)(2,1)} fusion(bf16[64,192,128]{2,0,1:T(8,128)(2,1)} %all-gather.3.cloned.1.call-done, s32[1024]{0:T(1024)S(1)} %pad_clamp_fusion.2), kind=kCustom, calls=%fused_computation.clone | custom fusion | bytes 6292224 | tf_op jit(solution)/shard_map/jit(_take)/gather | solution.py:38
  77.9 7.2 %fusion.2 = f32[48,64,128,1]{2,1,3,0:T(8,128)} fusion(bf16[48,6,128,128]{3,2,1,0:T(8,128)(2,1)} %param.12, bf16[48,4,64,128]{3,2,1,0:T(8,128)(2,1)} %bitcast.83, pred[48,4]{1,0:T(8,128)(4,1)S(1)} %copy.47), kind=kOutput, calls=%fused_computation.8 | convolution fusion | flops 404226048 | bytes 11010240 | tf_op jit(solution)/shard_map/rjab,prjb->pra/dot_general | solution.py:39
  85.2 17.2 %all-to-all-done = bf16[64,64,3,128]{3,0,2,1:T(8,128)(2,1)S(1)} async-done(((bf16[64,64,3,128]{3,0,2,1:T(8,128)(2,1)}), bf16[64,64,3,128]{3,0,2,1:T(8,128)(2,1)S(1)}, u32[]{:S(2)}, u32[]{:S(2)}) %all-to-all-start) | async-done | bytes 3145760 | tf_op jit(solution)/shard_map/all_to_all | solution.py:22
  102.4 1.9 gather_fusion.2
  104.3 4.1 %fusion.36 = bf16[64,48,128]{2,0,1:T(8,128)(2,1)S(1)} fusion(bf16[48,6,128,128]{3,2,1,0:T(8,128)(2,1)} %param.12, bf16[48,2,64,128]{3,2,1,0:T(8,128)(2,1)} %bitcast.84, pred[48,2]{1,0:T(8,128)(4,1)S(1)} %copy.50, f32[48,64,128,1]{2,1,3,0:T(8,128)} %fusion.2), kind=kOutput, calls=%fused_computation.43 | convolution fusion | flops 202899456 | bytes 7077984 | tf_op jit(solution)/shard_map/rjab,prjb->pra/dot_general | solution.py:45
  108.4 2.7 %gather_fusion.4 = bf16[192,64,128]{2,1,0:T(8,128)(2,1)} fusion(bf16[64,48,128]{2,0,1:T(8,128)(2,1)S(1)} %fusion.36, s32[1024]{0:T(1024)S(1)} %pad_clamp_fusion.1), kind=kCustom, calls=%fused_computation.4.clone | custom fusion | bytes 6292224 | tf_op jit(solution)/shard_map/jit(_take)/gather | solution.py:20
  111.2 3.3 %bitcast_select_fusion = bf16[64,64,3,128]{3,0,2,1:T(8,128)(2,1)} fusion(bf16[64,3,64,128]{3,2,1,0:T(8,128)(2,1)} %bitcast.77, pred[64,3]{1,0:T(8,128)(4,1)S(1)} %copy.51, pred[64,3]{1,0:T(8,128)(4,1)S(1)} %iota_compare_fusion), kind=kLoop, calls=%fused_computation.10 | loop fusion | flops 3145728 | bytes 6291840 | tf_op jit(solution)/shard_map/jit(_where)/select_n | solution.py:21
  114.5 5.3 %all-to-all-start.1 = ((bf16[64,64,3,128]{3,0,2,1:T(8,128)(2,1)}), bf16[64,64,3,128]{3,0,2,1:T(8,128)(2,1)S(1)}, u32[]{:S(2)}, u32[]{:S(2)}) async-start(bf16[64,64,3,128]{3,0,2,1:T(8,128)(2,1)} %bitcast_select_fusion), calls=%async_computation.1 | async-start | bytes 6291456 | tf_op jit(solution)/shard_map/all_to_all | solution.py:22
  119.9 0.7 all-gather.5.cloned.1.call-update
  120.6 44.0 %all-gather.5.cloned.1.call-done = bf16[64,192,128]{2,0,1:T(8,128)(2,1)} async-done(((bf16[64,48,128]{2,0,1:T(8,128)(2,1)}), bf16[64,192,128]{2,0,1:T(8,128)(2,1)}) %all-gather.5.cloned.1.call-update) | async-done | bytes 3145744 | tf_op jit(solution)/shard_map/all_gather | solution.py:37
  164.6 4.6 %gather_fusion.3 = bf16[192,64,128]{2,1,0:T(8,128)(2,1)} fusion(bf16[64,192,128]{2,0,1:T(8,128)(2,1)} %all-gather.5.cloned.1.call-done, s32[1024]{0:T(1024)S(1)} %pad_clamp_fusion.2), kind=kCustom, calls=%fused_computation.3.clone | custom fusion | bytes 6292224 | tf_op jit(solution)/shard_map/jit(_take)/gather | solution.py:38
  169.2 7.2 %fusion = f32[48,64,128,1]{2,1,3,0:T(8,128)} fusion(bf16[48,6,128,128]{3,2,1,0:T(8,128)(2,1)} %param.12, bf16[48,4,64,128]{3,2,1,0:T(8,128)(2,1)} %bitcast.82, pred[48,4]{1,0:T(8,128)(4,1)S(1)} %copy.47), kind=kOutput, calls=%fused_computation.6 | convolution fusion | flops 404226048 | bytes 11010240 | tf_op jit(solution)/shard_map/rjab,prjb->pra/dot_general | solution.py:39
  176.4 17.2 %all-to-all-done.1 = bf16[64,64,3,128]{3,0,2,1:T(8,128)(2,1)S(1)} async-done(((bf16[64,64,3,128]{3,0,2,1:T(8,128)(2,1)}), bf16[64,64,3,128]{3,0,2,1:T(8,128)(2,1)S(1)}, u32[]{:S(2)}, u32[]{:S(2)}) %all-to-all-start.1) | async-done | bytes 3145760 | tf_op jit(solution)/shard_map/all_to_all | solution.py:22
  193.7 1.9 gather_fusion.5
  195.6 4.2 %fusion.18 = f32[48,8,8,128]{3,2,1,0:T(8,128)S(1)} fusion(f32[48,64,128,1]{2,1,3,0:T(8,128)} %fusion, bf16[48,6,128,128]{3,2,1,0:T(8,128)(2,1)} %param.12, bf16[48,2,64,128]{3,2,1,0:T(8,128)(2,1)} %bitcast.81, pred[48,2]{1,0:T(8,128)(4,1)S(1)} %copy.50), kind=kOutput, calls=%fused_computation.31 | convolution fusion | flops 202899456 | bytes 7864416 | tf_op jit(solution)/shard_map/rjab,prjb->pra/dot_general | solution.py:45
  199.8 0.6 fusion.14
  200.5 0.7 pad_maximum_fusion
  (26 shorter events, 0.4 us)
Async XLA Ops:
  9.3 3.9 %copy-start = (bf16[64,48,128]{2,0,1:T(8,128)(2,1)}, bf16[64,48,128]{2,0,1:T(8,128)(2,1)S(1)}, u32[]{:S(2)}) copy-start(bf16[64,48,128]{2,0,1:T(8,128)(2,1)S(1)} %copy_bitcast_fusion) | copy-start | bytes 2359300
  16.5 12.8 %copy-start.5 = (s32[48,2]{0,1:T(2,128)S(1)}, s32[48,2]{0,1:T(2,128)}, u32[]{:S(2)}) copy-start(s32[48,2]{0,1:T(2,128)} %param.14) | copy-start | bytes 1156
  16.5 13.1 %copy-start.4 = (s32[48,4]{0,1:T(4,128)S(1)}, s32[48,4]{0,1:T(4,128)}, u32[]{:S(2)}) copy-start(s32[48,4]{0,1:T(4,128)} %param.13) | copy-start | bytes 2308
  16.5 85.9 %all-to-all-start = ((bf16[64,64,3,128]{3,0,2,1:T(8,128)(2,1)}), bf16[64,64,3,128]{3,0,2,1:T(8,128)(2,1)S(1)}, u32[]{:S(2)}, u32[]{:S(2)}) async-start(bf16[64,64,3,128]{3,0,2,1:T(8,128)(2,1)} %bitcast_select_fusion.1), calls=%async_computation | async-start | bytes 6291456 | tf_op jit(solution)/shard_map/all_to_all | solution.py:22
  28.5 44.8 %all-gather.3.cloned.1.call-start = ((), (), s32[]{:S(2)}) async-start(), calls=%async_computation.2 | async-start | bytes 3932160 | tf_op jit(solution)/shard_map/all_gather | solution.py:37
  108.4 2.8 %copy-start.1 = (bf16[64,48,128]{2,0,1:T(8,128)(2,1)}, bf16[64,48,128]{2,0,1:T(8,128)(2,1)S(1)}, u32[]{:S(2)}) copy-start(bf16[64,48,128]{2,0,1:T(8,128)(2,1)S(1)} %fusion.36) | copy-start | bytes 2359300
  114.5 79.1 %all-to-all-start.1 = ((bf16[64,64,3,128]{3,0,2,1:T(8,128)(2,1)}), bf16[64,64,3,128]{3,0,2,1:T(8,128)(2,1)S(1)}, u32[]{:S(2)}, u32[]{:S(2)}) async-start(bf16[64,64,3,128]{3,0,2,1:T(8,128)(2,1)} %bitcast_select_fusion), calls=%async_computation.1 | async-start | bytes 6291456 | tf_op jit(solution)/shard_map/all_to_all | solution.py:22
  119.8 44.8 %all-gather.5.cloned.1.call-start = ((), (), s32[]{:S(2)}) async-start(), calls=%async_computation.3 | async-start | bytes 3932160 | tf_op jit(solution)/shard_map/all_gather | solution.py:37
  195.6 4.2 %copy-start.2 = (bf16[64,48,128]{2,0,1:T(8,128)(2,1)S(1)}, bf16[64,48,128]{2,0,1:T(8,128)(2,1)}, u32[]{:S(2)}) copy-start(bf16[64,48,128]{2,0,1:T(8,128)(2,1)} %copy-done.1) | copy-start | bytes 2359300
  195.6 4.2 %copy-start.3 = (bf16[64,6144]{1,0:T(8,128)(2,1)S(1)}, bf16[64,6144]{1,0:T(8,128)(2,1)}, u32[]{:S(2)}) copy-start(bf16[64,6144]{1,0:T(8,128)(2,1)} %param.17) | copy-start | bytes 2359300
Sparse Core Ops, SparseCore 0:
  31.2 42.0 all-gather.2
  122.4 42.0 all-gather.4
where the time goes:
time: 208 us
  waiting for transfers between devices  123 us (59%)
  matrix products  22.7 us (11%)
  local copies, waits for them, and re-layouts  21 us (10%)
  starting transfers between devices  17.4 us (8%)
  between operations  13.6 us (7%)
  other arithmetic  10.1 us (5%)
    all_gather x2, waiting for transfers between devices, local_part(): panel_all = lax.all_gather(own, 'grp', axis=1, tiled=True)  87.3 us
    all_to_all x2, waiting for transfers between devices, send_boundary(): lax.all_to_all(outgoing, 'dom', split_axis=1, concat_axis=1, tiled=True)  34.4 us
    all_to_all x2, starting transfers between devices, send_boundary(): lax.all_to_all(outgoing, 'dom', split_axis=1, concat_axis=1, tiled=True)  17.3 us
    dot_general x2, matrix products, local_part(): jnp.einsum('rjab,prjb->pra', local_blocks, picked, preferred_element_type...  14.5 us
    gather x2, local copies, waits for them, and re-layouts, local_part(): picked = jnp.take(panel_all, local_cols, axis=1)  9.29 us
    dot_general x2, matrix products, remote_part(): jnp.einsum('rjab,prjb->pra', remote_blocks, picked, preferred_element_typ...  8.29 us
    select_n x2, other arithmetic, send_boundary(): jnp.where(live[None, :, :, None], outgoing, jnp.zeros_like(outgoing))  6.68 us
    gather x2, local copies, waits for them, and re-layouts, send_boundary(): outgoing = jnp.take(own, send_list, axis=1)  5.5 us
  transfers between devices with their start and end apart: 4, of which 4 were waited for; matrix products, arithmetic and copies ran while one was open for 12% of the time, Pallas kernels for 0%

commit v1 on v0

--- a/solution.py
+++ b/solution.py
@@ -34,7 +34,9 @@
     live = slot_index[None, :] < send_counts[0, 0][:, None]
 
     def local_part(own):
-        panel_all = lax.all_gather(own, "grp", axis=1, tiled=True)
+        panel_all = jnp.concatenate(
+            lax.all_to_all(jnp.stack([own] * lax.axis_size("grp")), "grp", 0, 0), axis=1
+        )
         picked = jnp.take(panel_all, local_cols, axis=1)
         return jnp.einsum(
             "rjab,prjb->pra", local_blocks, picked, preferred_element_type=jnp.float32

time: 208 us -> 271 us (1.30); the launches traced: 208 us -> 268 us
  waiting for transfers between devices: 123 us -> 168 us
  starting transfers between devices: 17.4 us -> 33.5 us
  local copies, waits for them, and re-layouts: 21 us -> 36.8 us
  between operations: 13.6 us -> 0.23 us
    all_gather x2 -> x0, waiting for transfers between devices: 87.3 us -> none  [local_part(): panel_all = lax.all_gather(own, 'grp', axis=1, tiled=True)]
    all_to_all x2, waiting for transfers between devices: 34.4 us -> 113 us  [send_boundary(): lax.all_to_all(outgoing, 'dom', split_axis=1, concat_axis=1, tiled=True)]
    all_to_all x0 -> x2, waiting for transfers between devices: none -> 54.1 us  [local_part(): lax.all_to_all(jnp.stack([own] * lax.axis_size('grp')), 'grp', 0, 0)]
    all_to_all x0 -> x2, starting transfers between devices: none -> 14.3 us  [local_part(): lax.all_to_all(jnp.stack([own] * lax.axis_size('grp')), 'grp', 0, 0)]
    all_to_all x0 -> x2, local copies, waits for them, and re-layouts: none -> 5.7 us  [local_part(): lax.all_to_all(jnp.stack([own] * lax.axis_size('grp')), 'grp', 0, 0)]
    another operation x0 -> x3, local copies, waits for them, and re-layouts: none -> 4.4 us  [local_part(): jnp.stack([own] * lax.axis_size('grp'))]
    reshape x1 -> x2, local copies, waits for them, and re-layouts: 1.34 us -> 5.71 us  [local_part(): jnp.concatenate(lax.all_to_all(jnp.stack([own] * lax.axis_size('grp')), '...]
  transfers between devices with their start and end apart: 4 -> 4, of which waited for: 4 -> 4; matrix products, arithmetic and copies ran while one was open for 12% -> 17% of each run, Pallas kernels for 0% -> 0%
where the time goes in v1:
time: 271 us; the launch traced here: 268 us
  waiting for transfers between devices  168 us (62%)
  local copies, waits for them, and re-layouts  36.8 us (14%)
  starting transfers between devices  33.5 us (12%)
  matrix products  21.8 us (8%)
  other arithmetic  8.13 us (3%)
    all_to_all x2, waiting for transfers between devices, send_boundary(): lax.all_to_all(outgoing, 'dom', split_axis=1, concat_axis=1, tiled=True)  113 us
    all_to_all x2, waiting for transfers between devices, local_part(): lax.all_to_all(jnp.stack([own] * lax.axis_size('grp')), 'grp', 0, 0)  54.1 us
    all_to_all x2, starting transfers between devices, send_boundary(): lax.all_to_all(outgoing, 'dom', split_axis=1, concat_axis=1, tiled=True)  19.1 us
    dot_general x2, matrix products, local_part(): jnp.einsum('rjab,prjb->pra', local_blocks, picked, preferred_element_type...  14.5 us
    all_to_all x2, starting transfers between devices, local_part(): lax.all_to_all(jnp.stack([own] * lax.axis_size('grp')), 'grp', 0, 0)  14.3 us
    gather x2, local copies, waits for them, and re-layouts, local_part(): picked = jnp.take(panel_all, local_cols, axis=1)  7.38 us
    dot_general x2, matrix products, remote_part(): jnp.einsum('rjab,prjb->pra', remote_blocks, picked, preferred_element_typ...  7.3 us
    select_n x2, other arithmetic, send_boundary(): jnp.where(live[None, :, :, None], outgoing, jnp.zeros_like(outgoing))  6.7 us
  transfers between devices with their start and end apart: 4, of which 4 were waited for; matrix products, arithmetic and copies ran while one was open for 17% of the time, Pallas kernels for 0%

profile of v1, /device:TPU:16, one launch (start us, length us, event | category | flops | bytes accessed | tf_op | source)
XLA Modules:
  0.0 268.0 jit_solution(9184374917667646811)
XLA Ops:
  0.0 1.3 copy.81
  1.3 2.1 stack.12
  3.4 6.8 %all-to-all-start = ((bf16[4,64,48,128]{3,2,1,0:T(8,128)(2,1)}), bf16[4,64,48,128]{3,2,1,0:T(8,128)(2,1)}, u32[]{:S(2)}, u32[]{:S(2)}) async-start(bf16[4,64,48,128]{3,2,1,0:T(8,128)(2,1)} %stack.12), calls=%async_computation | async-start | bytes 6291456 | tf_op jit(solution)/shard_map/all_to_all | solution.py:38
  10.2 0.1 reshape.168
  10.5 0.2 copy_bitcast_fusion
  10.8 2.7 %gather_fusion.1 = bf16[192,64,128]{2,1,0:T(8,128)(2,1)} fusion(bf16[64,48,128]{2,0,1:T(8,128)(2,1)S(1)} %copy_bitcast_fusion, s32[1024]{0:T(1024)S(1)} %pad_clamp_fusion.1), kind=kCustom, calls=%fused_computation.1.clone | custom fusion | bytes 6292224 | tf_op jit(solution)/shard_map/jit(_take)/gather | solution.py:20
  13.6 3.4 %bitcast_select_fusion.1 = bf16[64,64,3,128]{3,0,2,1:T(8,128)(2,1)} fusion(bf16[64,3,64,128]{3,2,1,0:T(8,128)(2,1)} %bitcast.86, pred[64,3]{1,0:T(8,128)(4,1)S(1)} %copy.58, pred[64,3]{1,0:T(8,128)(4,1)S(1)} %iota_compare_fusion), kind=kLoop, calls=%fused_computation.12 | loop fusion | flops 3145728 | bytes 6291840 | tf_op jit(solution)/shard_map/jit(_where)/select_n | solution.py:21
  16.9 26.4 %all-to-all-done = bf16[4,64,48,128]{3,2,1,0:T(8,128)(2,1)} async-done(((bf16[4,64,48,128]{3,2,1,0:T(8,128)(2,1)}), bf16[4,64,48,128]{3,2,1,0:T(8,128)(2,1)}, u32[]{:S(2)}, u32[]{:S(2)}) %all-to-all-start) | async-done | bytes 3145760 | tf_op jit(solution)/shard_map/all_to_all | solution.py:38
  43.3 12.3 %all-to-all-start.1 = ((bf16[64,64,3,128]{3,0,2,1:T(8,128)(2,1)}), bf16[64,64,3,128]{3,0,2,1:T(8,128)(2,1)}, u32[]{:S(2)}, u32[]{:S(2)}) async-start(bf16[64,64,3,128]{3,0,2,1:T(8,128)(2,1)} %bitcast_select_fusion.1), calls=%async_computation.1 | async-start | bytes 6291456 | tf_op jit(solution)/shard_map/all_to_all | solution.py:22
  56.3 2.8 %copy.54 = bf16[4,64,48,128]{3,2,0,1:T(8,128)(2,1)S(1)} copy(bf16[4,64,48,128]{3,2,1,0:T(8,128)(2,1)} %all-to-all-done) | data formatting | bytes 6291456 | tf_op jit(solution)/shard_map/all_to_all | solution.py:38
  59.2 2.0 copy.56
  61.2 2.7 %gather_fusion = bf16[192,64,128]{2,1,0:T(8,128)(2,1)} fusion(bf16[64,192,128]{2,0,1:T(8,128)(2,1)S(1)} %copy.56, s32[1024]{0:T(1024)S(1)} %pad_clamp_fusion.2), kind=kCustom, calls=%fused_computation.clone | custom fusion | bytes 6292224 | tf_op jit(solution)/shard_map/jit(_take)/gather | solution.py:40
  63.9 7.2 %fusion.2 = f32[48,64,128,1]{2,1,3,0:T(8,128)} fusion(bf16[48,6,128,128]{3,2,1,0:T(8,128)(2,1)} %param.12, bf16[48,4,64,128]{3,2,1,0:T(8,128)(2,1)} %bitcast.92, pred[48,4]{1,0:T(8,128)(4,1)S(1)} %copy.53), kind=kOutput, calls=%fused_computation.8 | convolution fusion | flops 404226048 | bytes 11010240 | tf_op jit(solution)/shard_map/rjab,prjb->pra/dot_general | solution.py:41
  71.2 58.1 %all-to-all-done.1 = bf16[64,64,3,128]{3,0,2,1:T(8,128)(2,1)} async-done(((bf16[64,64,3,128]{3,0,2,1:T(8,128)(2,1)}), bf16[64,64,3,128]{3,0,2,1:T(8,128)(2,1)}, u32[]{:S(2)}, u32[]{:S(2)}) %all-to-all-start.1) | async-done | bytes 3145760 | tf_op jit(solution)/shard_map/all_to_all | solution.py:22
  129.3 2.7 %gather_fusion.2 = bf16[96,64,128]{2,1,0:T(8,128)(2,1)S(1)} fusion(bf16[64,192,128]{2,0,1:T(8,128)(2,1)} %bitcast.10, s32[1024]{0:T(1024)S(1)} %pad_clamp_fusion), kind=kCustom, calls=%fused_computation.2.clone | custom fusion | bytes 3146112 | tf_op jit(solution)/shard_map/jit(_take)/gather | solution.py:46
  132.1 3.6 %fusion.36 = bf16[64,48,128]{2,0,1:T(8,128)(2,1)S(1)} fusion(bf16[48,6,128,128]{3,2,1,0:T(8,128)(2,1)} %param.12, bf16[48,2,64,128]{3,2,1,0:T(8,128)(2,1)S(1)} %bitcast.94, pred[48,2]{1,0:T(8,128)(4,1)S(1)} %copy.57, f32[48,64,128,1]{2,1,3,0:T(8,128)} %fusion.2), kind=kOutput, calls=%fused_computation.43 | convolution fusion | flops 202899456 | bytes 7077984 | tf_op jit(solution)/shard_map/rjab,prjb->pra/dot_general | solution.py:47
  135.7 0.5 copy.64
  136.2 2.1 stack.13
  138.3 7.6 %all-to-all-start.2 = ((bf16[4,64,48,128]{3,2,1,0:T(8,128)(2,1)}), bf16[4,64,48,128]{3,2,1,0:T(8,128)(2,1)}, u32[]{:S(2)}, u32[]{:S(2)}) async-start(bf16[4,64,48,128]{3,2,1,0:T(8,128)(2,1)} %stack.13), calls=%async_computation.2 | async-start | bytes 6291456 | tf_op jit(solution)/shard_map/all_to_all | solution.py:38
  145.9 2.7 %gather_fusion.4 = bf16[192,64,128]{2,1,0:T(8,128)(2,1)} fusion(bf16[64,48,128]{2,0,1:T(8,128)(2,1)S(1)} %fusion.36, s32[1024]{0:T(1024)S(1)} %pad_clamp_fusion.1), kind=kCustom, calls=%fused_computation.4.clone | custom fusion | bytes 6292224 | tf_op jit(solution)/shard_map/jit(_take)/gather | solution.py:20
  148.6 3.3 %bitcast_select_fusion = bf16[64,64,3,128]{3,0,2,1:T(8,128)(2,1)} fusion(bf16[64,3,64,128]{3,2,1,0:T(8,128)(2,1)} %bitcast.85, pred[64,3]{1,0:T(8,128)(4,1)S(1)} %copy.58, pred[64,3]{1,0:T(8,128)(4,1)S(1)} %iota_compare_fusion), kind=kLoop, calls=%fused_computation.10 | loop fusion | flops 3145728 | bytes 6291840 | tf_op jit(solution)/shard_map/jit(_where)/select_n | solution.py:21
  151.9 27.7 %all-to-all-done.2 = bf16[4,64,48,128]{3,2,1,0:T(8,128)(2,1)} async-done(((bf16[4,64,48,128]{3,2,1,0:T(8,128)(2,1)}), bf16[4,64,48,128]{3,2,1,0:T(8,128)(2,1)}, u32[]{:S(2)}, u32[]{:S(2)}) %all-to-all-start.2) | async-done | bytes 3145760 | tf_op jit(solution)/shard_map/all_to_all | solution.py:38
  179.6 6.8 %all-to-all-start.3 = ((bf16[64,64,3,128]{3,0,2,1:T(8,128)(2,1)}), bf16[64,64,3,128]{3,0,2,1:T(8,128)(2,1)}, u32[]{:S(2)}, u32[]{:S(2)}) async-start(bf16[64,64,3,128]{3,0,2,1:T(8,128)(2,1)} %bitcast_select_fusion), calls=%async_computation.3 | async-start | bytes 6291456 | tf_op jit(solution)/shard_map/all_to_all | solution.py:22
  186.5 2.8 %copy.65 = bf16[4,64,48,128]{3,2,0,1:T(8,128)(2,1)S(1)} copy(bf16[4,64,48,128]{3,2,1,0:T(8,128)(2,1)} %all-to-all-done.2) | data formatting | bytes 6291456 | tf_op jit(solution)/shard_map/all_to_all | solution.py:38
  189.3 3.7 %copy.67 = bf16[64,192,128]{2,0,1:T(8,128)(2,1)} copy(bf16[64,192,128]{2,1,0:T(8,128)(2,1)S(1)} %bitcast.88) | data formatting | bytes 6291456 | tf_op jit(solution)/shard_map/reshape | solution.py:37
  193.0 4.6 %gather_fusion.3 = bf16[192,64,128]{2,1,0:T(8,128)(2,1)} fusion(bf16[64,192,128]{2,0,1:T(8,128)(2,1)} %copy.67, s32[1024]{0:T(1024)S(1)} %pad_clamp_fusion.2), kind=kCustom, calls=%fused_computation.3.clone | custom fusion | bytes 6292224 | tf_op jit(solution)/shard_map/jit(_take)/gather | solution.py:40
  197.6 7.2 %fusion = f32[48,64,128,1]{2,1,3,0:T(8,128)} fusion(bf16[48,6,128,128]{3,2,1,0:T(8,128)(2,1)} %param.12, bf16[48,4,64,128]{3,2,1,0:T(8,128)(2,1)} %bitcast.91, pred[48,4]{1,0:T(8,128)(4,1)S(1)} %copy.53), kind=kOutput, calls=%fused_computation.6 | convolution fusion | flops 404226048 | bytes 11010240 | tf_op jit(solution)/shard_map/rjab,prjb->pra/dot_general | solution.py:41
  204.9 55.3 %all-to-all-done.3 = bf16[64,64,3,128]{3,0,2,1:T(8,128)(2,1)} async-done(((bf16[64,64,3,128]{3,0,2,1:T(8,128)(2,1)}), bf16[64,64,3,128]{3,0,2,1:T(8,128)(2,1)}, u32[]{:S(2)}, u32[]{:S(2)}) %all-to-all-start.3) | async-done | bytes 3145760 | tf_op jit(solution)/shard_map/all_to_all | solution.py:22
  260.2 2.7 %gather_fusion.5 = bf16[96,64,128]{2,1,0:T(8,128)(2,1)S(1)} fusion(bf16[64,192,128]{2,0,1:T(8,128)(2,1)} %bitcast.25, s32[1024]{0:T(1024)S(1)} %pad_clamp_fusion), kind=kCustom, calls=%fused_computation.5.clone | custom fusion | bytes 3146112 | tf_op jit(solution)/shard_map/jit(_take)/gather | solution.py:46
  263.0 3.7 %fusion.18 = f32[48,8,8,128]{3,2,1,0:T(8,128)S(1)} fusion(f32[48,64,128,1]{2,1,3,0:T(8,128)} %fusion, bf16[48,6,128,128]{3,2,1,0:T(8,128)(2,1)} %param.12, bf16[48,2,64,128]{3,2,1,0:T(8,128)(2,1)S(1)} %bitcast.90, pred[48,2]{1,0:T(8,128)(4,1)S(1)} %copy.57), kind=kOutput, calls=%fused_computation.31 | convolution fusion | flops 202899456 | bytes 7864416 | tf_op jit(solution)/shard_map/rjab,prjb->pra/dot_general | solution.py:47
  266.7 0.6 fusion.14
  267.3 0.7 pad_maximum_fusion
  (32 shorter events, 1.0 us)
Async XLA Ops:
  3.4 6.8 %copy-start.3 = (s32[1,1,64,3]{2,1,3,0:T(1,128)S(1)}, s32[1,1,64,3]{2,1,3,0:T(1,128)}, u32[]{:S(2)}) copy-start(s32[1,1,64,3]{2,1,3,0:T(1,128)} %param.15) | copy-start | bytes 2308
  3.4 7.2 %copy-start = (bf16[64,6144]{1,0:T(8,128)(2,1)S(1)}, bf16[64,6144]{1,0:T(8,128)(2,1)}, u32[]{:S(2)}) copy-start(bf16[64,6144]{1,0:T(8,128)(2,1)} %param.17) | copy-start | bytes 2359300
  3.4 39.9 %all-to-all-start = ((bf16[4,64,48,128]{3,2,1,0:T(8,128)(2,1)}), bf16[4,64,48,128]{3,2,1,0:T(8,128)(2,1)}, u32[]{:S(2)}, u32[]{:S(2)}) async-start(bf16[4,64,48,128]{3,2,1,0:T(8,128)(2,1)} %stack.12), calls=%async_computation | async-start | bytes 6291456 | tf_op jit(solution)/shard_map/all_to_all | solution.py:38
  10.8 2.7 %copy-start.5 = (s32[1,1,64]{2,1,0:T(1,128)S(1)}, s32[1,1,64]{2,1,0:T(1,128)}, u32[]{:S(2)}) copy-start(s32[1,1,64]{2,1,0:T(1,128)} %param.16) | copy-start | bytes 772
  16.9 38.7 %copy-start.4 = (s32[48,2]{0,1:T(2,128)S(1)}, s32[48,2]{0,1:T(2,128)}, u32[]{:S(2)}) copy-start(s32[48,2]{0,1:T(2,128)} %param.14) | copy-start | bytes 1156
  16.9 38.9 %copy-start.2 = (s32[48,4]{0,1:T(4,128)S(1)}, s32[48,4]{0,1:T(4,128)}, u32[]{:S(2)}) copy-start(s32[48,4]{0,1:T(4,128)} %param.13) | copy-start | bytes 2308
  43.3 86.0 %all-to-all-start.1 = ((bf16[64,64,3,128]{3,0,2,1:T(8,128)(2,1)}), bf16[64,64,3,128]{3,0,2,1:T(8,128)(2,1)}, u32[]{:S(2)}, u32[]{:S(2)}) async-start(bf16[64,64,3,128]{3,0,2,1:T(8,128)(2,1)} %bitcast_select_fusion.1), calls=%async_computation.1 | async-start | bytes 6291456 | tf_op jit(solution)/shard_map/all_to_all | solution.py:22
  138.3 41.4 %all-to-all-start.2 = ((bf16[4,64,48,128]{3,2,1,0:T(8,128)(2,1)}), bf16[4,64,48,128]{3,2,1,0:T(8,128)(2,1)}, u32[]{:S(2)}, u32[]{:S(2)}) async-start(bf16[4,64,48,128]{3,2,1,0:T(8,128)(2,1)} %stack.13), calls=%async_computation.2 | async-start | bytes 6291456 | tf_op jit(solution)/shard_map/all_to_all | solution.py:38
  179.6 80.6 %all-to-all-start.3 = ((bf16[64,64,3,128]{3,0,2,1:T(8,128)(2,1)}), bf16[64,64,3,128]{3,0,2,1:T(8,128)(2,1)}, u32[]{:S(2)}, u32[]{:S(2)}) async-start(bf16[64,64,3,128]{3,0,2,1:T(8,128)(2,1)} %bitcast_select_fusion), calls=%async_computation.3 | async-start | bytes 6291456 | tf_op jit(solution)/shard_map/all_to_all | solution.py:22
  262.9 3.7 %copy-start.1 = (bf16[64,6144]{1,0:T(8,128)(2,1)S(1)}, bf16[64,6144]{1,0:T(8,128)(2,1)}, u32[]{:S(2)}) copy-start(bf16[64,6144]{1,0:T(8,128)(2,1)} %param.17) | copy-start | bytes 2359300
